TPU v7x, 512 devices: a whole 4x4x16 slice. The times are simulated.
512 devices in a mesh: space: 64 (over z, x), radial: 8 (over y, core).
Axes of the slice: x: 4, y: 4, z: 16, core: 2. Of those that a mesh axis runs over, the one named last changes fastest.
Arguments:
- snapshots: float32 [32, 5, 1024, 1024], P(None, None, 'space', 'radial'), as said below
Outputs:
- modes: float32 [32, 5, 1024, 1024], P(None, None, 'space', 'radial')
- divergence: float32 [32, 5, 1024, 1024], P(None, None, 'space', 'radial')
- reduced: float32 [32, 32], replicated
Inputs may be any that keep to these rules, and one draw needn't show every extreme that they name: `snapshots`: density (variable 0) lies between 0.5 and 1.5; energy (variable 4) exceeds the kinetic energy by 1 or more.
All inputs are finite; a program needn't handle non-finite values.
Results may differ from a plain program's by a relative error of at most 0.0003.
Values sent between devices are 32-bit elements; how exact they have to be, the bound alone decides.
A program may use at most 64 MiB of HBM per device.

v0:
```python
import jax
import jax.numpy as jnp
from jax import lax
from jax.sharding import PartitionSpec as P


def padded_2(block, sides, width):
    for axis, dim in sides:
        count = lax.axis_size(axis)
        forward = [(i, i + 1) for i in range(count - 1)]
        backward = [(target, source) for source, target in forward]
        low = lax.ppermute(
            lax.slice_in_dim(block, block.shape[dim] - width, None, axis=dim), axis, forward
        )
        high = lax.ppermute(lax.slice_in_dim(block, 0, width, axis=dim), axis, backward)
        block = jnp.concatenate([low, block, high], axis=dim)
    return block


def flux_pair(snapshots):
    rho = snapshots[:, 0]
    mom_a = snapshots[:, 1]
    mom_b = snapshots[:, 2]
    mom_c = snapshots[:, 3]
    energy = snapshots[:, 4]
    speed_a = mom_a / rho
    speed_b = mom_b / rho
    press = 0.4 * (energy - 0.5 * (mom_a * speed_a + mom_b * speed_b + mom_c * mom_c / rho))
    axial = jnp.stack(
        [
            mom_a,
            mom_a * speed_a + press,
            mom_b * speed_a,
            mom_c * speed_a,
            (energy + press) * speed_a,
        ],
        1,
    )
    radial = jnp.stack(
        [
            mom_b,
            mom_a * speed_b,
            mom_b * speed_b + press,
            mom_c * speed_b,
            (energy + press) * speed_b,
        ],
        1,
    )
    return (axial, radial)


def central(padded, dim, count):
    coeffs = (0.75, -0.15, 1.0 / 60.0)
    total = jnp.zeros_like(lax.slice_in_dim(padded, 3, 3 + count, axis=dim))
    for step in range(3):
        ahead = lax.slice_in_dim(padded, 3 + step + 1, 3 + step + 1 + count, axis=dim)
        behind = lax.slice_in_dim(padded, 3 - step - 1, 3 - step - 1 + count, axis=dim)
        total = total + coeffs[step] * (ahead - behind)
    return total


def per_device(snapshots):
    hp = lax.Precision.HIGHEST
    width = snapshots.shape[1]
    axial_len = snapshots.shape[2]
    radial_len = snapshots.shape[3]
    axial, radial = flux_pair(snapshots)
    pad_a = padded_2(axial, (("space", 2),), 3)
    pad_r = padded_2(radial, (("radial", 3),), 3)
    divergence = -(central(pad_a, 2, axial_len) + central(pad_r, 3, radial_len))
    count = width * axial_len * lax.axis_size("space") * radial_len * lax.axis_size("radial")
    root = jnp.sqrt(jnp.float32(count))
    local_gram = jnp.einsum("svxr,tvxr->st", snapshots, snapshots, precision=hp)
    identity = jnp.eye(local_gram.shape[0], dtype=jnp.float32)
    gram = lax.psum(local_gram, ("space", "radial"))
    factor = jnp.linalg.cholesky(gram / count)
    lower = lax.linalg.triangular_solve(factor, identity, left_side=True, lower=True)
    modes = jnp.einsum("ks,svxr->kvxr", lower, snapshots, precision=hp)
    local_red = jnp.einsum("kvxr,jvxr->kj", modes, divergence, precision=hp)
    reduced = lax.psum(local_red, ("space", "radial")) / root
    return (modes, divergence, reduced)


def solution(mesh):
    placed = (P(None, None, "space", "radial"),)
    return jax.shard_map(
        per_device,
        mesh=mesh,
        in_specs=placed,
        out_specs=(P(None, None, "space", "radial"), P(None, None, "space", "radial"), P()),
        check_vma=False,
    )
```

profile of v0, /device:TPU:1, one launch (start us, length us, event | category | flops | bytes accessed | tf_op | source)
XLA Modules:
  0.0 263.6 jit_solution(2122451710394651808)
XLA Ops:
  0.6 1.7 copy.11
  2.4 0.1 multiply_dynamic-update-slice_fusion.2
  2.5 0.2 add_dynamic-update-slice_fusion
  2.6 0.1 add_dynamic-update-slice_fusion.1
  2.8 0.1 multiply_dynamic-update-slice_fusion.1
  2.8 0.1 multiply_dynamic-update-slice_fusion
  2.9 0.0 copy-start.1
  2.9 1.0 copy-done.1
  4.0 1.5 fusion.32
  5.5 0.6 copy.21
  6.1 0.0 copy-start
  6.1 8.9 %collective-permute-start.2 = (f32[32,5,16,3]{0,2,3,1:T(8,128)S(1)}, f32[32,5,16,3]{0,2,3,1:T(8,128)}, u32[]{:S(2)}, u32[]{:S(2)}) collective-permute-start(f32[32,5,16,3]{0,2,3,1:T(8,128)S(1)} %copy.21), channel_id=1, source_target_pairs={{1,0},{2,1},{3,2},{4,3},{5,4},{6,5},{7,6},{9,8},{10,9},{11,10},{12... | collective-permute-start | bytes 92168 | tf_op jit(solution)/shard_map/ppermute | solution.py:15
  15.0 2.5 copy.23
  17.5 1.9 collective-permute-start.3
  19.4 1.8 fusion.33
  21.2 1.3 collective-permute-start
  22.5 4.0 %collective-permute-start.1 = (f32[32,5,3,128]{3,0,2,1:T(8,128)S(1)}, f32[32,5,3,128]{3,0,2,1:T(8,128)S(1)}, u32[]{:S(2)}, u32[]{:S(2)}) collective-permute-start(f32[32,5,3,128]{3,0,2,1:T(8,128)S(1)} %get-tuple-element.21), channel_id=1, source_target_pairs={{0,8},{8,16},{16,24},{24,32},{32,40},{40,48},{48,56},{56,64},{64,7... | collective-permute-start | bytes 737288 | tf_op jit(solution)/shard_map/ppermute | solution.py:12
  26.5 0.0 copy-done
  26.5 1.4 convolution_bitcast_fusion.2
  28.0 108.5 %psum.14 = f32[32,32]{0,1:T(8,128)S(1)} all-reduce(f32[32,32]{0,1:T(8,128)S(1)} %convolution_bitcast_fusion.2), channel_id=1, replica_groups=mesh['space'=64,'radial'=8] {'space','radial'}, use_global_device_ids=true, to_apply=%region_0.0 | all-reduce | flops 1024 | bytes 8192 | tf_op jit(solution)/shard_map/psum | solution.py:75
  136.5 0.1 copy.14
  136.6 2.9 %cholesky.17 = f32[32,32]{1,0:T(8,128)S(1)} custom-call(f32[32,32]{1,0:T(8,128)S(1)} %fusion.28), custom_call_target="Cholesky" | custom-call | tf_op jit(solution)/shard_map/jit(cholesky)/cholesky | solution.py:76
  139.5 0.6 compare_reduce_fusion
  140.2 0.7 fusion.26
  140.8 2.4 custom-call.6
  143.3 0.2 convolution_bitcast_fusion
  143.5 2.8 %fusion.29 = f32[32,5,16,128]{3,0,2,1:T(8,128)S(1)} fusion(f32[32,32,1,1]{1,0,3,2:T(8,128)S(1)} %convolution_bitcast_fusion, f32[32,5,16,128]{3,2,1,0:T(8,128)} %param.1), kind=kOutput, calls=%fused_computation.76 | convolution fusion | flops 125829120 | bytes 2625536 | tf_op jit(solution)/shard_map/ks,svxr->kvxr/dot_general | solution.py:78
  146.3 1.8 copy.25
  148.1 0.0 collective-permute-done.2
  148.1 2.5 copy.22
  150.6 0.0 collective-permute-done.3
  150.6 2.5 copy.24
  153.2 0.0 collective-permute-done
  153.2 0.0 collective-permute-done.1
  153.2 7.9 %fusion.6 = f32[32,5,16,128]{3,0,2,1:T(8,128)S(1)} fusion(f32[32,5,16,128]{3,0,2,1:T(8,128)} %copy-done.1, f32[32,5,3,128]{3,0,2,1:T(8,128)S(1)} %collective-permute-done.1, f32[32,5,3,128]{3,0,2,1:T(8,128)S(1)} %collective-permute-done, f32[32,5,16,3]{3,0,2,1:T(8,128)} %copy.24, f32[32,5,16,128]{3,0,2,1:T(8,128)S(1)} %get-tuple-element.14, ...), kind=kLoop, calls=%fused_computation.22 | loop fusion | flops 9830400 | bytes 4485120 | tf_op jit(solution)/shard_map/neg | solution.py:70
  161.1 1.2 convolution_bitcast_fusion.1
  162.3 1.8 copy.26
  164.1 98.8 %psum.15 = f32[32,32]{1,0:T(8,128)S(1)} all-reduce(f32[32,32]{1,0:T(8,128)S(1)} %convolution_bitcast_fusion.1), channel_id=1, replica_groups=mesh['space'=64,'radial'=8] {'space','radial'}, use_global_device_ids=true, to_apply=%region_3.4 | all-reduce | flops 1024 | bytes 8192 | tf_op jit(solution)/shard_map/psum | solution.py:80
  263.0 0.6 broadcast_multiply_fusion
  (5 shorter events, 0.1 us)
Async XLA Ops:
  2.9 1.1 copy-start.1
  6.1 20.4 %copy-start = (f32[32,5,16,128]{3,2,1,0:T(8,128)S(1)}, f32[32,5,16,128]{3,2,1,0:T(8,128)}, u32[]{:S(2)}) copy-start(f32[32,5,16,128]{3,2,1,0:T(8,128)} %param.1) | copy-start | bytes 3932164
  6.1 142.0 %collective-permute-start.2 = (f32[32,5,16,3]{0,2,3,1:T(8,128)S(1)}, f32[32,5,16,3]{0,2,3,1:T(8,128)}, u32[]{:S(2)}, u32[]{:S(2)}) collective-permute-start(f32[32,5,16,3]{0,2,3,1:T(8,128)S(1)} %copy.21), channel_id=1, source_target_pairs={{1,0},{2,1},{3,2},{4,3},{5,4},{6,5},{7,6},{9,8},{10,9},{11,10},{12... | collective-permute-start | bytes 92168 | tf_op jit(solution)/shard_map/ppermute | solution.py:15
  17.5 133.1 %collective-permute-start.3 = (f32[32,5,16,3]{0,2,3,1:T(8,128)}, f32[32,5,16,3]{0,2,3,1:T(8,128)}, u32[]{:S(2)}, u32[]{:S(2)}) collective-permute-start(f32[32,5,16,3]{0,2,3,1:T(8,128)} %copy.23), channel_id=1, source_target_pairs={{0,1},{1,2},{2,3},{3,4},{4,5},{5,6},{6,7},{8,9},{9,10},{10,11},{11... | collective-permute-start | bytes 92168 | tf_op jit(solution)/shard_map/ppermute | solution.py:12
  21.2 131.9 %collective-permute-start = (f32[32,5,3,128]{3,0,2,1:T(8,128)}, f32[32,5,3,128]{3,0,2,1:T(8,128)S(1)}, u32[]{:S(2)}, u32[]{:S(2)}) collective-permute-start(f32[32,5,3,128]{3,0,2,1:T(8,128)} %get-tuple-element.20), channel_id=1, source_target_pairs={{8,0},{16,8},{24,16},{32,24},{40,32},{48,40},{56,48},{64,56},{72,6... | collective-permute-start | bytes 737288 | tf_op jit(solution)/shard_map/ppermute | solution.py:15
  22.5 130.6 %collective-permute-start.1 = (f32[32,5,3,128]{3,0,2,1:T(8,128)S(1)}, f32[32,5,3,128]{3,0,2,1:T(8,128)S(1)}, u32[]{:S(2)}, u32[]{:S(2)}) collective-permute-start(f32[32,5,3,128]{3,0,2,1:T(8,128)S(1)} %get-tuple-element.21), channel_id=1, source_target_pairs={{0,8},{8,16},{16,24},{24,32},{32,40},{40,48},{48,56},{56,64},{64,7... | collective-permute-start | bytes 737288 | tf_op jit(solution)/shard_map/ppermute | solution.py:12
where the time goes:
time: 264 us
  blocking collectives  207 us (78%)
  local copies, waits for them, and re-layouts  18 us (7%)
  starting transfers between devices  16.1 us (6%)
  other arithmetic  15.7 us (6%)
  matrix products  5.61 us (2%)
    psum x1, blocking collectives, per_device(): gram = lax.psum(local_gram, ('space', 'radial'))  108 us
    psum x1, blocking collectives, per_device(): reduced = lax.psum(local_red, ('space', 'radial')) / root  98.8 us
    ppermute x2, starting transfers between devices, padded_2(): lax.ppermute(lax.slice_in_dim(block, 0, width, axis=dim), axis, backward)  10.2 us
    neg x1, other arithmetic, per_device(): divergence = -(central(pad_a, 2, axial_len) + central(pad_r, 3, radial_len))  7.92 us
    unnamed x8, local copies, waits for them, and re-layouts  6.45 us
    ppermute x2, starting transfers between devices, padded_2(): lax.ppermute(lax.slice_in_dim(block, block.shape[dim] - width, None, axis...  5.91 us
  transfers between devices with their start and end apart: 4, of which 0 were waited for; matrix products, arithmetic and copies ran while one was open for 9% of the time, Pallas kernels for 0%

commit v1 on v0

v1 whole, which is shorter than its diff:
```python
import functools
import itertools

import jax
import jax.numpy as jnp
from jax import lax
from jax.experimental import pallas as pl
from jax.experimental.pallas import tpu as pltpu
from jax.sharding import PartitionSpec as P

MESH = pl.DeviceIdType.MESH
F32 = jnp.float32
BF16 = jnp.bfloat16
HIGHEST = lax.Precision.HIGHEST
COEFFS = (0.75, -0.15, 1.0 / 60.0)
S, V, NI, NL = 32, 5, 16, 128
EDGE = (0, 1, 2, 13, 14, 15)
NT = (((1,), (1,)), ((), ()))
TN = (((0,), (0,)), ((), ()))


def split(a):
    high = a.astype(BF16)
    low = (a - high.astype(F32)).astype(BF16)
    return jnp.concatenate([high, low], axis=0)


def flux_state(q):
    rho, ma, mb, mc, energy = q
    inv = 1.0 / rho
    ua, ub, uc = ma * inv, mb * inv, mc * inv
    press = 0.4 * (energy - 0.5 * (ma * ua + mb * ub + mc * uc))
    return ua, ub, press


def flux_axial(q):
    _, ma, mb, mc, energy = q
    ua, _, press = flux_state(q)
    return (ma, ma * ua + press, mb * ua, mc * ua, (energy + press) * ua)


def flux_radial(q):
    _, ma, mb, mc, energy = q
    _, ub, press = flux_state(q)
    return (mb, ma * ub, mb * ub + press, mc * ub, (energy + press) * ub)


def flux_both(q):
    _, ma, mb, mc, energy = q
    ua, ub, press = flux_state(q)
    cross, total = mb * ua, energy + press
    axial = (ma, ma * ua + press, cross, mc * ua, total * ua)
    radial = (mb, cross, mb * ub + press, mc * ub, total * ub)
    return axial, radial


def pack(acc, tmp):
    tmp[...] = jnp.zeros_like(tmp)
    tmp[:, 0:64] = acc
    full = tmp[...]
    rows = full[0:32] + full[32:64]
    both = rows + pltpu.roll(rows, NL - 32, axis=1)
    lane = lax.broadcasted_iota(jnp.int32, (8, NL), 1)
    out = jnp.zeros((8, NL), F32)
    for r in range(4):
        part = both[8 * r : 8 * r + 8]
        if r:
            part = pltpu.roll(part, 32 * r, axis=1)
        out = jnp.where(lane // 32 == r, part, out)
    return out


def unpack(tile):
    return jnp.concatenate([tile] + [pltpu.roll(tile, NL - 32 * r, axis=1) for r in (1, 2, 3)], axis=0)


def inverse_factor(gram):
    row = lax.broadcasted_iota(jnp.int32, (S, NL), 0)
    lane = lax.broadcasted_iota(jnp.int32, (S, NL), 1)
    w = jnp.where(lane < S, gram, jnp.where(lane == row + S, 1.0, 0.0))
    for k in range(S - 1):
        pivot = w[k : k + 1, :]
        scale = w[:, k : k + 1] * (1.0 / w[k : k + 1, k : k + 1])
        w = w - jnp.where(row > k, scale, 0.0) * pivot
    diag = jnp.sum(jnp.where(lane == row, w, 0.0), axis=1, keepdims=True)
    low = pltpu.roll(w, NL - S, axis=1) * lax.rsqrt(diag)
    return jnp.where(lane < S, low, 0.0)


def ring(d, n):
    return min(d, n - d)


def main_kernel(dims, count, snap, modes, div, red, y, yp, fs, dt, mt, ed, ha, hr, tmp, sb, rc, rp, rz, load_sem, out_sem, send, recv):
    nz, nx, ny = dims
    nsp, nra = nz * nx, ny * 2
    sp, ra = lax.axis_index("space"), lax.axis_index("radial")
    z, x = sp // nx, sp % nx
    yy, c = ra // 2, ra % 2
    plane_offsets = sorted(
        [o for o in itertools.product(range(nx), range(ny)) if any(o)], key=lambda o: -ring(o[0], nx) - ring(o[1], ny)
    )
    deep_offsets = sorted(range(1, nz), key=lambda d: -ring(d, nz))

    def plane(o):
        return (z * nx + (x + o[0]) % nx, ((yy + o[1]) % ny) * 2 + c)

    def deep(d):
        return (((z + d) % nz) * nx + x, ra)

    core = (sp, yy * 2 + 1 - c)
    ahead_a, behind_a = ((sp + 1) % nsp, ra), ((sp + nsp - 1) % nsp, ra)
    ahead_r, behind_r = (sp, (ra + 1) % nra), (sp, (ra + nra - 1) % nra)

    barrier = pltpu.get_barrier_semaphore()
    peers = [deep(d) for d in deep_offsets] + [plane(o) for o in plane_offsets] + [core, ahead_a, behind_a, ahead_r, behind_r]
    for peer in peers:
        pl.semaphore_signal(barrier, inc=1, device_id=peer, device_id_type=MESH)
    for s in range(S):
        pltpu.make_async_copy(snap.at[s], y.at[:, :, s, :], load_sem).start()
    pltpu.make_async_copy(y, y, load_sem).wait()
    pl.semaphore_wait(barrier, len(peers))

    def remote(src, dst, k, peer):
        return pltpu.make_async_remote_copy(src, dst, send.at[k], recv.at[k], device_id=peer, device_id_type=MESH)

    halo = [remote(y.at[:, NI - 3 : NI], ha.at[0], 0, ahead_a), remote(y.at[:, 0:3], ha.at[1], 1, behind_a)]
    for h in halo:
        h.start()

    def start_core(k, tile):
        sb[3 * k] = tile
        remote(sb.at[3 * k], rc.at[k], 4 + 3 * k, core).start()

    def end_core(k):
        remote(sb.at[3 * k], rc.at[k], 4 + 3 * k, core).wait()
        return sb[3 * k] + rc[k]

    def start_many(k, stage, buf, mine, targets, tile):
        sb[3 * k + stage] = tile
        buf[k, mine] = tile
        for peer in targets:
            remote(sb.at[3 * k + stage], buf.at[k, mine], 4 + 3 * k + stage, peer).start()

    def end_many(k, stage, buf, n):
        landed = buf.at[k, 0 : n - 1]
        pltpu.make_async_copy(landed, landed, recv.at[4 + 3 * k + stage]).wait()
        pltpu.make_async_copy(landed, landed, send.at[4 + 3 * k + stage]).wait()
        parts = [buf[k, i] for i in range(n)]
        while len(parts) > 1:
            parts = [parts[i] + parts[i + 1] for i in range(0, len(parts), 2)]
        return parts[0]

    def start_plane(k, tile):
        start_many(k, 1, rp, x * ny + yy, [plane(o) for o in plane_offsets], tile)

    def end_plane(k):
        return end_many(k, 1, rp, nx * ny)

    def start_deep(k, tile):
        start_many(k, 2, rz, z, [deep(d) for d in deep_offsets], tile)

    def end_deep(k):
        return end_many(k, 2, rz, nz)

    def gram_step(v, acc):
        for i in range(NI):
            p = split(y[v, i])
            yp[v, i] = p
            acc = acc + lax.dot_general(p, p, NT, preferred_element_type=F32)
        return acc

    acc = lax.fori_loop(0, V, gram_step, jnp.zeros((2 * S, 2 * S), F32))
    start_core(0, pack(acc, tmp))

    row8 = lax.broadcasted_iota(jnp.int32, (8, NL), 0)
    lane8 = lax.broadcasted_iota(jnp.int32, (8, NL), 1)
    pick = jnp.where((row8 < 6) & (lane8 == jnp.where(row8 < 3, row8, row8 + NL - 6)), 1.0, 0.0)

    def edge_step(v, carry):
        for j in range(4):
            rows = y[v, 4 * j : 4 * j + 4].reshape(4 * S, NL)
            ed[v, j] = lax.dot_general(pick, rows, NT, preferred_element_type=F32, precision=HIGHEST)
        return carry

    lax.fori_loop(0, V, edge_step, 0)
    radial_halo = [remote(ed, hr.at[0], 2, ahead_r), remote(ed, hr.at[1], 3, behind_r)]
    for h in radial_halo:
        h.start()

    start_plane(0, end_core(0))

    lane1 = lax.broadcasted_iota(jnp.int32, (1, NL), 1)
    up = [jnp.where(lane1 + k < NL, cf, 0.0) for k, cf in zip((1, 2, 3), COEFFS)]
    down = [jnp.where(lane1 >= k, cf, 0.0) for k, cf in zip((1, 2, 3), COEFFS)]

    def flux_step(i, carry):
        axial, radial = flux_both([y[v, i] for v in range(V)])
        for v in range(V):
            fs[v, 3 + i] = axial[v]
            g = radial[v]
            total = jnp.zeros_like(g)
            for k in (1, 2, 3):
                total = total + (down[k - 1] * pltpu.roll(g, k, axis=1) - up[k - 1] * pltpu.roll(g, NL - k, axis=1))
            dt[v, i] = total
        return carry

    lax.fori_loop(0, NI, flux_step, 0)

    for h in radial_halo:
        h.wait()
    row = lax.broadcasted_iota(jnp.int32, (8, NL), 0)
    hs = []
    for v in range(V):
        cells = [jnp.where(row < 3, hr[1, v, j], hr[0, v, j]) for j in range(4)]
        if v == 0:
            cells = [jnp.where(row < 6, a, 1.0) for a in cells]
        hs.append(cells)
    valid = jnp.where(row < 3, jnp.where(ra < nra - 1, 1, 0), jnp.where((row < 6) & (ra > 0), 1, 0)) > 0
    step = jnp.where(row8 < 3, row8 + NL - lane8, lane8 + 6 - row8)
    weight = jnp.zeros((8, NL), F32)
    for k, cf in zip((1, 2, 3), COEFFS):
        weight = jnp.where(step == k, cf, weight)
    weight = jnp.where(row8 < 6, jnp.where(row8 < 3, -weight, weight), 0.0)
    edge_flux = [flux_radial([hs[v][j] for v in range(V)]) for j in range(4)]
    for v in range(V):
        for j in range(4):
            g = jnp.where(valid, edge_flux[j][v], 0.0)
            add = lax.dot_general(g, weight, TN, preferred_element_type=F32, precision=HIGHEST)
            dt[v, 4 * j : 4 * j + 4] = dt[v, 4 * j : 4 * j + 4] + add.reshape(4, S, NL)

    def axial_row(v, i):
        total = jnp.zeros((S, NL), F32)
        for k, cf in zip((1, 2, 3), COEFFS):
            total = total + cf * (fs[v, i + 3 - k] - fs[v, i + 3 + k])
        d = dt[v, i] + total
        dt[v, i] = d
        return lax.dot_general(yp[v, i], split(d), NT, preferred_element_type=F32)

    def inner_step(i, acc):
        for v in range(V):
            acc = acc + axial_row(v, i)
        return acc

    acc = lax.fori_loop(3, NI - 3, inner_step, jnp.zeros((2 * S, 2 * S), F32), unroll=2)

    start_deep(0, end_plane(0))

    for h in halo:
        h.wait()
    for side in range(2):
        keep = jnp.full((S, NL), jnp.where(sp > 0, 1, 0) if side == 0 else jnp.where(sp < nsp - 1, 1, 0)) > 0
        for j in range(3):
            axial = flux_axial([ha[side, v, j] for v in range(V)])
            for v in range(V):
                fs[v, j + (NI + 3) * side] = jnp.where(keep, axial[v], 0.0)
    for i in EDGE:
        acc = inner_step(i, acc)
    start_core(1, pack(acc, tmp))
    for s in range(S):
        pltpu.make_async_copy(dt.at[:, :, s, :], div.at[s], out_sem.at[0]).start()
    start_plane(1, end_core(1))
    gram = unpack(end_deep(0)) / count
    start_deep(1, end_plane(1))
    low = inverse_factor(gram)

    twice = low + pltpu.roll(low, S, axis=1)
    high = twice.astype(BF16)
    lhs = jnp.concatenate([high, (twice - high.astype(F32)).astype(BF16)], axis=0)[:, 0 : 2 * S]

    def mode_step(v, carry):
        for i in range(NI):
            out = jnp.dot(lhs, yp[v, i], preferred_element_type=F32)
            mt[v, i] = out[0:S] + out[S : 2 * S]
        return carry

    lax.fori_loop(0, V, mode_step, 0)
    for s in range(S):
        pltpu.make_async_copy(mt.at[:, :, s, :], modes.at[s], out_sem.at[1]).start()
    cross = unpack(end_deep(1))
    root = jnp.sqrt(jnp.full((S, S), count, F32))
    red[...] = jnp.dot(low[:, 0:S], cross[:, 0:S], preferred_element_type=F32, precision=HIGHEST) / root
    pltpu.make_async_copy(dt, dt, out_sem.at[0]).wait()
    pltpu.make_async_copy(mt, mt, out_sem.at[1]).wait()


def per_device(dims, snapshots):
    nz, nx, ny = dims
    count = float(V * NI * nz * nx * NL * ny * 2)
    vmem = pl.BlockSpec(memory_space=pltpu.VMEM)
    hbm = pl.BlockSpec(memory_space=pl.ANY)
    big = (S, V, NI, NL)
    dma = pltpu.SemaphoreType.DMA
    modes, div, red = pl.pallas_call(
        functools.partial(main_kernel, dims, count),
        out_shape=[pltpu.VMEM(big, F32), pltpu.VMEM(big, F32), pltpu.VMEM((S, S), F32)],
        in_specs=[hbm],
        out_specs=[vmem, vmem, vmem],
        scratch_shapes=[
            pltpu.VMEM((V, NI, S, NL), F32),
            pltpu.VMEM((V, NI, 2 * S, NL), BF16),
            pltpu.VMEM((V, NI + 6, S, NL), F32),
            pltpu.VMEM((V, NI, S, NL), F32),
            pltpu.VMEM((V, NI, S, NL), F32),
            pltpu.VMEM((V, 4, 8, NL), F32),
            pltpu.VMEM((2, V, 3, S, NL), F32),
            pltpu.VMEM((2, V, 4, 8, NL), F32),
            pltpu.VMEM((2 * S, NL), F32),
            pltpu.VMEM((6, 8, NL), F32),
            pltpu.VMEM((2, 8, NL), F32),
            pltpu.VMEM((2, nx * ny, 8, NL), F32),
            pltpu.VMEM((2, nz, 8, NL), F32),
            dma,
            dma((2,)),
            dma((10,)),
            dma((10,)),
        ],
        compiler_params=pltpu.CompilerParams(collective_id=0, has_side_effects=True),
    )(snapshots)
    return modes, div, red


def solution(mesh):
    space, radial = mesh.shape["space"], mesh.shape["radial"]
    nx = 4 if space > 4 else 2
    placed = P(None, None, "space", "radial")
    return jax.shard_map(
        functools.partial(per_device, (space // nx, nx, radial // 2)),
        mesh=mesh,
        in_specs=(placed,),
        out_specs=(placed, placed, P()),
        check_vma=False,
    )
```

time: 264 us -> 46.6 us (0.18)
  the two profiles are of different devices: /device:TPU:1 before, /device:TPU:6 now
where the time goes in v1:
time: 46.6 us; the launch traced here: 46.3 us
  Pallas kernels  43 us (92%)
  local copies, waits for them, and re-layouts  2.72 us (6%)
  between operations  0.64 us (1%)
    pallas_call x1, Pallas kernels, per_device(): pl.pallas_call(functools.partial(main_kernel, dims, count), out_shape=[pl...  43 us
    unnamed x3, local copies, waits for them, and re-layouts  2.72 us

profile of v1, /device:TPU:6, one launch (start us, length us, event | category | flops | bytes accessed | tf_op | source)
XLA Modules:
  0.0 46.3 jit_solution(9056753454775493119)
XLA Ops:
  0.6 43.0 %shard_map.38 = (f32[32,5,16,128]{3,2,1,0:T(8,128)S(1)}, f32[32,5,16,128]{3,2,1,0:T(8,128)S(1)}, f32[32,32]{1,0:T(8,128)S(1)}) custom-call(f32[32,5,16,128]{3,2,1,0:T(8,128)} %snap.1), custom_call_target="tpu_custom_call" | custom-call | tf_op jit(solution)/shard_map/pallas_call | solution.py:294
  43.6 1.1 %copy.7 = f32[32,5,16,128]{3,2,1,0:T(8,128)} copy(f32[32,5,16,128]{3,2,1,0:T(8,128)S(1)} %get-tuple-element.3) | data formatting | bytes 2621440
  44.7 0.6 %copy.9 = f32[32,32]{1,0:T(8,128)} copy(f32[32,32]{1,0:T(8,128)S(1)} %get-tuple-element.5) | data formatting | bytes 8192
  45.3 1.1 %copy.8 = f32[32,5,16,128]{3,2,1,0:T(8,128)} copy(f32[32,5,16,128]{3,2,1,0:T(8,128)S(1)} %get-tuple-element.4) | data formatting | bytes 2621440

commit v2 on v1

--- a/solution.py
+++ b/solution.py
@@ -23,6 +23,11 @@
     high = a.astype(BF16)
     low = (a - high.astype(F32)).astype(BF16)
     return jnp.concatenate([high, low], axis=0)
+
+
+def high_low(a):
+    high = a.astype(BF16)
+    return jnp.concatenate([high, (a - high.astype(F32)).astype(BF16)], axis=1)
 
 
 def flux_state(q):
@@ -91,7 +96,11 @@
     return min(d, n - d)
 
 
-def main_kernel(dims, count, snap, modes, div, red, y, yp, fs, dt, mt, ed, ha, hr, tmp, sb, rc, rp, rz, load_sem, out_sem, send, recv):
+def offsets(n, steps):
+    return sorted({d % n for k in steps for d in (k, -k)} - {0})
+
+
+def main_kernel(dims, count, snap, modes, div, red, y, yp, fs, dt, mt, gs, gt, ed, ha, hr, tmp, sb, rc, rp, rz, known, load_sem, out_sem, send, recv):
     nz, nx, ny = dims
     nsp, nra = nz * nx, ny * 2
     sp, ra = lax.axis_index("space"), lax.axis_index("radial")
@@ -113,13 +122,19 @@
     ahead_r, behind_r = (sp, (ra + 1) % nra), (sp, (ra + nra - 1) % nra)
 
     barrier = pltpu.get_barrier_semaphore()
-    peers = [deep(d) for d in deep_offsets] + [plane(o) for o in plane_offsets] + [core, ahead_a, behind_a, ahead_r, behind_r]
-    for peer in peers:
-        pl.semaphore_signal(barrier, inc=1, device_id=peer, device_id_type=MESH)
+    line_x, line_y = [plane((d, 0)) for d in range(1, nx)], [plane((0, d)) for d in range(1, ny)]
+    near_z, skip_z, far_z = [[deep(d) for d in offsets(nz, n)] for n in ((1, 2), (2,), (4,))]
+
+    def signal(semaphore, targets):
+        for peer in targets:
+            pl.semaphore_signal(semaphore, inc=1, device_id=peer, device_id_type=MESH)
+        return len(targets)
+
+    near = signal(barrier, [ahead_a, behind_a, ahead_r, behind_r, core] + near_z + line_x + line_y)
     for s in range(S):
         pltpu.make_async_copy(snap.at[s], y.at[:, :, s, :], load_sem).start()
     pltpu.make_async_copy(y, y, load_sem).wait()
-    pl.semaphore_wait(barrier, len(peers))
+    pl.semaphore_wait(barrier, near)
 
     def remote(src, dst, k, peer):
         return pltpu.make_async_remote_copy(src, dst, send.at[k], recv.at[k], device_id=peer, device_id_type=MESH)
@@ -127,6 +142,7 @@
     halo = [remote(y.at[:, NI - 3 : NI], ha.at[0], 0, ahead_a), remote(y.at[:, 0:3], ha.at[1], 1, behind_a)]
     for h in halo:
         h.start()
+    near = signal(known.at[0], line_x + skip_z)
 
     def start_core(k, tile):
         sb[3 * k] = tile
@@ -163,71 +179,80 @@
     def end_deep(k):
         return end_many(k, 2, rz, nz)
 
+    row8 = lax.broadcasted_iota(jnp.int32, (8, NL), 0)
+    lane8 = lax.broadcasted_iota(jnp.int32, (8, NL), 1)
+    row16 = lax.broadcasted_iota(jnp.int32, (16, NL), 0)
+    lane16 = lax.broadcasted_iota(jnp.int32, (16, NL), 1)
+    pick = jnp.where((row16 < 6) & (lane16 == jnp.where(row16 < 3, row16, row16 + NL - 6)), 1.0, 0.0).astype(BF16)
+
     def gram_step(v, acc):
-        for i in range(NI):
-            p = split(y[v, i])
-            yp[v, i] = p
-            acc = acc + lax.dot_general(p, p, NT, preferred_element_type=F32)
+        for j in range(4):
+            edge = []
+            for i in range(4 * j, 4 * j + 4):
+                p = split(y[v, i])
+                yp[v, i] = p
+                out = lax.dot_general(jnp.concatenate([p, pick], axis=0), p, NT, preferred_element_type=F32)
+                acc = acc + out[0 : 2 * S]
+                edge.append(out[2 * S : 2 * S + 8, 0:S] + out[2 * S : 2 * S + 8, S : 2 * S])
+            ed[v, j] = jnp.concatenate(edge, axis=1)
         return acc
 
     acc = lax.fori_loop(0, V, gram_step, jnp.zeros((2 * S, 2 * S), F32))
     start_core(0, pack(acc, tmp))
-
-    row8 = lax.broadcasted_iota(jnp.int32, (8, NL), 0)
-    lane8 = lax.broadcasted_iota(jnp.int32, (8, NL), 1)
-    pick = jnp.where((row8 < 6) & (lane8 == jnp.where(row8 < 3, row8, row8 + NL - 6)), 1.0, 0.0)
-
-    def edge_step(v, carry):
-        for j in range(4):
-            rows = y[v, 4 * j : 4 * j + 4].reshape(4 * S, NL)
-            ed[v, j] = lax.dot_general(pick, rows, NT, preferred_element_type=F32, precision=HIGHEST)
-        return carry
-
-    lax.fori_loop(0, V, edge_step, 0)
     radial_halo = [remote(ed, hr.at[0], 2, ahead_r), remote(ed, hr.at[1], 3, behind_r)]
     for h in radial_halo:
         h.start()
 
-    start_plane(0, end_core(0))
-
-    lane1 = lax.broadcasted_iota(jnp.int32, (1, NL), 1)
-    up = [jnp.where(lane1 + k < NL, cf, 0.0) for k, cf in zip((1, 2, 3), COEFFS)]
-    down = [jnp.where(lane1 >= k, cf, 0.0) for k, cf in zip((1, 2, 3), COEFFS)]
+    tile = end_core(0)
+    pl.semaphore_wait(known.at[0], near)
+    start_plane(0, tile)
+    far = signal(known.at[1], far_z)
 
     def flux_step(i, carry):
         axial, radial = flux_both([y[v, i] for v in range(V)])
         for v in range(V):
             fs[v, 3 + i] = axial[v]
-            g = radial[v]
-            total = jnp.zeros_like(g)
-            for k in (1, 2, 3):
-                total = total + (down[k - 1] * pltpu.roll(g, k, axis=1) - up[k - 1] * pltpu.roll(g, NL - k, axis=1))
-            dt[v, i] = total
+            high = radial[v].astype(BF16)
+            gs[v, i, :, 0:NL] = high
+            gs[v, i, :, NL : 2 * NL] = (radial[v] - high.astype(F32)).astype(BF16)
         return carry
 
     lax.fori_loop(0, NI, flux_step, 0)
+    shift = lax.broadcasted_iota(jnp.int32, (NL, NL), 1) - lax.broadcasted_iota(jnp.int32, (NL, NL), 0)
+    matrix = jnp.zeros((NL, NL), F32)
+    for k, cf in zip((1, 2, 3), COEFFS):
+        matrix = jnp.where(shift == k, cf, jnp.where(shift == -k, -cf, matrix))
+    matrix = high_low(matrix)
+    matrix = jnp.concatenate([matrix, matrix], axis=0)
+
+    def radial_step(v, carry):
+        out = jnp.dot(gs[v].reshape(NI * S, 2 * NL), matrix, preferred_element_type=F32)
+        dt[v] = (out[:, 0:NL] + out[:, NL : 2 * NL]).reshape(NI, S, NL)
+        return carry
+
+    lax.fori_loop(0, V, radial_step, 0)
 
     for h in radial_halo:
         h.wait()
-    row = lax.broadcasted_iota(jnp.int32, (8, NL), 0)
-    hs = []
-    for v in range(V):
-        cells = [jnp.where(row < 3, hr[1, v, j], hr[0, v, j]) for j in range(4)]
-        if v == 0:
-            cells = [jnp.where(row < 6, a, 1.0) for a in cells]
-        hs.append(cells)
-    valid = jnp.where(row < 3, jnp.where(ra < nra - 1, 1, 0), jnp.where((row < 6) & (ra > 0), 1, 0)) > 0
     step = jnp.where(row8 < 3, row8 + NL - lane8, lane8 + 6 - row8)
     weight = jnp.zeros((8, NL), F32)
     for k, cf in zip((1, 2, 3), COEFFS):
         weight = jnp.where(step == k, cf, weight)
     weight = jnp.where(row8 < 6, jnp.where(row8 < 3, -weight, weight), 0.0)
-    edge_flux = [flux_radial([hs[v][j] for v in range(V)]) for j in range(4)]
+    weights = high_low(jnp.concatenate([weight] * 16, axis=0))
+    group = (lax.broadcasted_iota(jnp.int32, (NL, 2 * NL), 0) // 8) % 8
+    valid = jnp.where(row8 < 3, jnp.where(ra < nra - 1, 1, 0), jnp.where((row8 < 6) & (ra > 0), 1, 0)) > 0
+    blank = jnp.zeros((24, NL), F32)
+    for j in range(4):
+        cells = [jnp.where(row8 < 3, hr[1, v, j], hr[0, v, j]) for v in range(V)]
+        cells[0] = jnp.where(row8 < 6, cells[0], 1.0)
+        rows = jnp.concatenate([jnp.where(valid, g, 0.0) for g in flux_radial(cells)], axis=0)
+        high = rows.astype(BF16).astype(F32)
+        rows = jnp.concatenate([high, blank, rows - high, blank], axis=0)
+        gt[j] = rows.T.astype(BF16)
     for v in range(V):
-        for j in range(4):
-            g = jnp.where(valid, edge_flux[j][v], 0.0)
-            add = lax.dot_general(g, weight, TN, preferred_element_type=F32, precision=HIGHEST)
-            dt[v, 4 * j : 4 * j + 4] = dt[v, 4 * j : 4 * j + 4] + add.reshape(4, S, NL)
+        out = jnp.dot(gt[...].reshape(NI * S, NL), jnp.where(group == v, weights, 0.0).astype(BF16), preferred_element_type=F32)
+        dt[v] = dt[v] + (out[:, 0:NL] + out[:, NL : 2 * NL]).reshape(NI, S, NL)
 
     def axial_row(v, i):
         total = jnp.zeros((S, NL), F32)
@@ -244,7 +269,10 @@
 
     acc = lax.fori_loop(3, NI - 3, inner_step, jnp.zeros((2 * S, 2 * S), F32), unroll=2)
 
-    start_deep(0, end_plane(0))
+    tile = end_plane(0)
+    if far:
+        pl.semaphore_wait(known.at[1], far)
+    start_deep(0, tile)
 
     for h in halo:
         h.wait()
@@ -282,6 +310,15 @@
     red[...] = jnp.dot(low[:, 0:S], cross[:, 0:S], preferred_element_type=F32, precision=HIGHEST) / root
     pltpu.make_async_copy(dt, dt, out_sem.at[0]).wait()
     pltpu.make_async_copy(mt, mt, out_sem.at[1]).wait()
+
+
+def write_kernel(modes, div, red, modes_out, div_out, red_out, sem):
+    pairs = ((modes, modes_out), (div, div_out), (red, red_out))
+    copies = [pltpu.make_async_copy(a, b, sem.at[i]) for i, (a, b) in enumerate(pairs)]
+    for copy in copies:
+        copy.start()
+    for copy in copies:
+        copy.wait()
 
 
 def per_device(dims, snapshots):
@@ -302,6 +339,8 @@
             pltpu.VMEM((V, NI + 6, S, NL), F32),
             pltpu.VMEM((V, NI, S, NL), F32),
             pltpu.VMEM((V, NI, S, NL), F32),
+            pltpu.VMEM((V, NI, S, 2 * NL), BF16),
+            pltpu.VMEM((4, NL, NL), BF16),
             pltpu.VMEM((V, 4, 8, NL), F32),
             pltpu.VMEM((2, V, 3, S, NL), F32),
             pltpu.VMEM((2, V, 4, 8, NL), F32),
@@ -310,6 +349,7 @@
             pltpu.VMEM((2, 8, NL), F32),
             pltpu.VMEM((2, nx * ny, 8, NL), F32),
             pltpu.VMEM((2, nz, 8, NL), F32),
+            pltpu.SemaphoreType.REGULAR((2,)),
             dma,
             dma((2,)),
             dma((10,)),
@@ -317,6 +357,14 @@
         ],
         compiler_params=pltpu.CompilerParams(collective_id=0, has_side_effects=True),
     )(snapshots)
+    pinned = [pltpu.with_memory_space_constraint(a, pltpu.VMEM) for a in (modes, div, red)]
+    modes, div, red = pl.pallas_call(
+        write_kernel,
+        out_shape=[jax.ShapeDtypeStruct(big, F32), jax.ShapeDtypeStruct(big, F32), jax.ShapeDtypeStruct((S, S), F32)],
+        in_specs=[vmem, vmem, vmem],
+        out_specs=[hbm, hbm, hbm],
+        scratch_shapes=[dma((3,))],
+    )(*pinned)
     return modes, div, red
 
 

time: 46.6 us -> 41.4 us (0.89)
  the two profiles are of different devices: /device:TPU:6 before, /device:TPU:1 now
where the time goes in v2:
time: 41.4 us; the launch traced here: 41.2 us
  Pallas kernels  40.6 us (98%)
  between operations  0.64 us (2%)
    pallas_call x1, Pallas kernels, per_device(): pl.pallas_call(functools.partial(main_kernel, dims, count), out_shape=[pl...  39.1 us
    pallas_call x1, Pallas kernels, per_device(): pl.pallas_call(write_kernel, out_shape=[jax.ShapeDtypeStruct(big, F32), j...  1.52 us

profile of v2, /device:TPU:1, one launch (start us, length us, event | category | flops | bytes accessed | tf_op | source)
XLA Modules:
  0.0 41.2 jit_solution(12082164087723149408)
XLA Ops:
  0.6 39.1 %shard_map.38 = (f32[32,5,16,128]{3,2,1,0:T(8,128)S(1)}, f32[32,5,16,128]{3,2,1,0:T(8,128)S(1)}, f32[32,32]{1,0:T(8,128)S(1)}) custom-call(f32[32,5,16,128]{3,2,1,0:T(8,128)} %snap.1), custom_call_target="tpu_custom_call" | custom-call | tf_op jit(solution)/shard_map/pallas_call | solution.py:331
  39.7 1.5 %shard_map.39 = (f32[32,5,16,128]{3,2,1,0:T(8,128)}, f32[32,5,16,128]{3,2,1,0:T(8,128)}, f32[32,32]{1,0:T(8,128)}) custom-call(f32[32,5,16,128]{3,2,1,0:T(8,128)S(1)} %get-tuple-element.6.modes, f32[32,5,16,128]{3,2,1,0:T(8,128)S(1)} %get-tuple-element.7.div, f32[32,32]{1,0:T(8,128)S(1)} %get-tuple-element.8.red), custom_call_target="tpu_custom_call" | custom-call | tf_op jit(solution)/shard_map/pallas_call | solution.py:361

commit v3 on v2

--- a/solution.py
+++ b/solution.py
@@ -1,5 +1,4 @@
 import functools
-import itertools
 
 import jax
 import jax.numpy as jnp
@@ -92,10 +91,6 @@
     return jnp.where(lane < S, low, 0.0)
 
 
-def ring(d, n):
-    return min(d, n - d)
-
-
 def offsets(n, steps):
     return sorted({d % n for k in steps for d in (k, -k)} - {0})
 
@@ -106,16 +101,20 @@
     sp, ra = lax.axis_index("space"), lax.axis_index("radial")
     z, x = sp // nx, sp % nx
     yy, c = ra // 2, ra % 2
-    plane_offsets = sorted(
-        [o for o in itertools.product(range(nx), range(ny)) if any(o)], key=lambda o: -ring(o[0], nx) - ring(o[1], ny)
-    )
-    deep_offsets = sorted(range(1, nz), key=lambda d: -ring(d, nz))
-
     def plane(o):
         return (z * nx + (x + o[0]) % nx, ((yy + o[1]) % ny) * 2 + c)
 
     def deep(d):
         return (((z + d) % nz) * nx + x, ra)
+
+    def nth_plane(n):
+        half_x, half_y = nx // 2, ny // 2
+        own = (nx - half_x) % nx * ny + (ny - half_y) % ny
+        n = jnp.where(n >= own, n + 1, n)
+        return plane((half_x + n // ny, half_y + n % ny))
+
+    def nth_deep(n):
+        return deep(nz // 2 + jnp.where(n % 2 == 1, nz - (n + 1) // 2, n // 2))
 
     core = (sp, yy * 2 + 1 - c)
     ahead_a, behind_a = ((sp + 1) % nsp, ra), ((sp + nsp - 1) % nsp, ra)
@@ -152,11 +151,15 @@
         remote(sb.at[3 * k], rc.at[k], 4 + 3 * k, core).wait()
         return sb[3 * k] + rc[k]
 
-    def start_many(k, stage, buf, mine, targets, tile):
+    def start_many(k, stage, buf, mine, n, target, tile):
         sb[3 * k + stage] = tile
         buf[k, mine] = tile
-        for peer in targets:
-            remote(sb.at[3 * k + stage], buf.at[k, mine], 4 + 3 * k + stage, peer).start()
+
+        def send_one(i, carry):
+            remote(sb.at[3 * k + stage], buf.at[k, mine], 4 + 3 * k + stage, target(i)).start()
+            return carry
+
+        lax.fori_loop(0, n - 1, send_one, 0)
 
     def end_many(k, stage, buf, n):
         landed = buf.at[k, 0 : n - 1]
@@ -168,13 +171,13 @@
         return parts[0]
 
     def start_plane(k, tile):
-        start_many(k, 1, rp, x * ny + yy, [plane(o) for o in plane_offsets], tile)
+        start_many(k, 1, rp, x * ny + yy, nx * ny, nth_plane, tile)
 
     def end_plane(k):
         return end_many(k, 1, rp, nx * ny)
 
     def start_deep(k, tile):
-        start_many(k, 2, rz, z, [deep(d) for d in deep_offsets], tile)
+        start_many(k, 2, rz, z, nz, nth_deep, tile)
 
     def end_deep(k):
         return end_many(k, 2, rz, nz)
@@ -203,10 +206,6 @@
     for h in radial_halo:
         h.start()
 
-    tile = end_core(0)
-    pl.semaphore_wait(known.at[0], near)
-    start_plane(0, tile)
-    far = signal(known.at[1], far_z)
 
     def flux_step(i, carry):
         axial, radial = flux_both([y[v, i] for v in range(V)])
@@ -218,6 +217,10 @@
         return carry
 
     lax.fori_loop(0, NI, flux_step, 0)
+    tile = end_core(0)
+    pl.semaphore_wait(known.at[0], near)
+    start_plane(0, tile)
+    far = signal(known.at[1], far_z)
     shift = lax.broadcasted_iota(jnp.int32, (NL, NL), 1) - lax.broadcasted_iota(jnp.int32, (NL, NL), 0)
     matrix = jnp.zeros((NL, NL), F32)
     for k, cf in zip((1, 2, 3), COEFFS):
@@ -285,11 +288,11 @@
     for i in EDGE:
         acc = inner_step(i, acc)
     start_core(1, pack(acc, tmp))
+    start_plane(1, end_core(1))
     for s in range(S):
         pltpu.make_async_copy(dt.at[:, :, s, :], div.at[s], out_sem.at[0]).start()
-    start_plane(1, end_core(1))
+    start_deep(1, end_plane(1))
     gram = unpack(end_deep(0)) / count
-    start_deep(1, end_plane(1))
     low = inverse_factor(gram)
 
     twice = low + pltpu.roll(low, S, axis=1)

time: 41.4 us -> 39.2 us (0.947)
  Pallas kernels: 40.6 us -> 38.4 us
    pallas_call x1, Pallas kernels: 39.1 us -> 36.8 us  [per_device(): pl.pallas_call(functools.partial(main_kernel, dims, count), out_shape=[pl...]
where the time goes in v3:
time: 39.2 us; the launch traced here: 39 us
  Pallas kernels  38.4 us (98%)
  between operations  0.64 us (2%)
    pallas_call x1, Pallas kernels, per_device(): pl.pallas_call(functools.partial(main_kernel, dims, count), out_shape=[pl...  36.8 us
    pallas_call x1, Pallas kernels, per_device(): pl.pallas_call(write_kernel, out_shape=[jax.ShapeDtypeStruct(big, F32), j...  1.52 us

profile of v3, /device:TPU:1, one launch (start us, length us, event | category | flops | bytes accessed | tf_op | source)
XLA Modules:
  0.0 39.0 jit_solution(9070933498696784718)
XLA Ops:
  0.6 36.8 %shard_map.38 = (f32[32,5,16,128]{3,2,1,0:T(8,128)S(1)}, f32[32,5,16,128]{3,2,1,0:T(8,128)S(1)}, f32[32,32]{1,0:T(8,128)S(1)}) custom-call(f32[32,5,16,128]{3,2,1,0:T(8,128)} %snap.1), custom_call_target="tpu_custom_call" | custom-call | tf_op jit(solution)/shard_map/pallas_call | solution.py:334
  37.5 1.5 %shard_map.39 = (f32[32,5,16,128]{3,2,1,0:T(8,128)}, f32[32,5,16,128]{3,2,1,0:T(8,128)}, f32[32,32]{1,0:T(8,128)}) custom-call(f32[32,5,16,128]{3,2,1,0:T(8,128)S(1)} %get-tuple-element.6.modes, f32[32,5,16,128]{3,2,1,0:T(8,128)S(1)} %get-tuple-element.7.div, f32[32,32]{1,0:T(8,128)S(1)} %get-tuple-element.8.red), custom_call_target="tpu_custom_call" | custom-call | tf_op jit(solution)/shard_map/pallas_call | solution.py:364

commit v4 on v3

--- a/solution.py
+++ b/solution.py
@@ -13,7 +13,6 @@
 HIGHEST = lax.Precision.HIGHEST
 COEFFS = (0.75, -0.15, 1.0 / 60.0)
 S, V, NI, NL = 32, 5, 16, 128
-EDGE = (0, 1, 2, 13, 14, 15)
 NT = (((1,), (1,)), ((), ()))
 TN = (((0,), (0,)), ((), ()))
 
@@ -95,7 +94,7 @@
     return sorted({d % n for k in steps for d in (k, -k)} - {0})
 
 
-def main_kernel(dims, count, snap, modes, div, red, y, yp, fs, dt, mt, gs, gt, ed, ha, hr, tmp, sb, rc, rp, rz, known, load_sem, out_sem, send, recv):
+def main_kernel(dims, count, snap, modes, div, red, y, yp, fs, fh, dt, mt, gs, gt, ed, ha, hr, tmp, sb, rc, rp, rz, known, load_sem, out_sem, send, recv):
     nz, nx, ny = dims
     nsp, nra = nz * nx, ny * 2
     sp, ra = lax.axis_index("space"), lax.axis_index("radial")
@@ -138,9 +137,9 @@
     def remote(src, dst, k, peer):
         return pltpu.make_async_remote_copy(src, dst, send.at[k], recv.at[k], device_id=peer, device_id_type=MESH)
 
-    halo = [remote(y.at[:, NI - 3 : NI], ha.at[0], 0, ahead_a), remote(y.at[:, 0:3], ha.at[1], 1, behind_a)]
-    for h in halo:
-        h.start()
+    first_halo = remote(y.at[:, pl.ds((1 - c) * (NI - 3), 3)], ha.at[c], 0, ((sp + nsp + 1 - 2 * c) % nsp, ra))
+    other_halo = remote(y.at[:, pl.ds(c * (NI - 3), 3)], ha.at[1 - c], 1, ((sp + nsp - 1 + 2 * c) % nsp, ra))
+    first_halo.start()
     near = signal(known.at[0], line_x + skip_z)
 
     def start_core(k, tile):
@@ -184,19 +183,22 @@
 
     row8 = lax.broadcasted_iota(jnp.int32, (8, NL), 0)
     lane8 = lax.broadcasted_iota(jnp.int32, (8, NL), 1)
-    row16 = lax.broadcasted_iota(jnp.int32, (16, NL), 0)
-    lane16 = lax.broadcasted_iota(jnp.int32, (16, NL), 1)
-    pick = jnp.where((row16 < 6) & (lane16 == jnp.where(row16 < 3, row16, row16 + NL - 6)), 1.0, 0.0).astype(BF16)
+    row16 = lax.broadcasted_iota(jnp.int32, (16, 2 * NL), 0)
+    lane16 = lax.broadcasted_iota(jnp.int32, (16, 2 * NL), 1)
+    cell = row16 % 8
+    pick = (cell < 6) & (lane16 == row16 // 8 * NL + jnp.where(cell < 3, cell, cell + NL - 6))
+    pick = jnp.where(pick, 1.0, 0.0).astype(BF16)
 
     def gram_step(v, acc):
         for j in range(4):
             edge = []
-            for i in range(4 * j, 4 * j + 4):
-                p = split(y[v, i])
+            for i in (2 * j, 2 * j + 1):
+                p = split(jnp.concatenate([y[v, 2 * i], y[v, 2 * i + 1]], axis=1))
                 yp[v, i] = p
                 out = lax.dot_general(jnp.concatenate([p, pick], axis=0), p, NT, preferred_element_type=F32)
                 acc = acc + out[0 : 2 * S]
-                edge.append(out[2 * S : 2 * S + 8, 0:S] + out[2 * S : 2 * S + 8, S : 2 * S])
+                for r in (2 * S, 2 * S + 8):
+                    edge.append(out[r : r + 8, 0:S] + out[r : r + 8, S : 2 * S])
             ed[v, j] = jnp.concatenate(edge, axis=1)
         return acc
 
@@ -210,7 +212,7 @@
     def flux_step(i, carry):
         axial, radial = flux_both([y[v, i] for v in range(V)])
         for v in range(V):
-            fs[v, 3 + i] = axial[v]
+            fs[v, i] = axial[v]
             high = radial[v].astype(BF16)
             gs[v, i, :, 0:NL] = high
             gs[v, i, :, NL : 2 * NL] = (radial[v] - high.astype(F32)).astype(BF16)
@@ -221,6 +223,7 @@
     pl.semaphore_wait(known.at[0], near)
     start_plane(0, tile)
     far = signal(known.at[1], far_z)
+    other_halo.start()
     shift = lax.broadcasted_iota(jnp.int32, (NL, NL), 1) - lax.broadcasted_iota(jnp.int32, (NL, NL), 0)
     matrix = jnp.zeros((NL, NL), F32)
     for k, cf in zip((1, 2, 3), COEFFS):
@@ -257,38 +260,74 @@
         out = jnp.dot(gt[...].reshape(NI * S, NL), jnp.where(group == v, weights, 0.0).astype(BF16), preferred_element_type=F32)
         dt[v] = dt[v] + (out[:, 0:NL] + out[:, NL : 2 * NL]).reshape(NI, S, NL)
 
-    def axial_row(v, i):
-        total = jnp.zeros((S, NL), F32)
-        for k, cf in zip((1, 2, 3), COEFFS):
-            total = total + cf * (fs[v, i + 3 - k] - fs[v, i + 3 + k])
-        d = dt[v, i] + total
-        dt[v, i] = d
-        return lax.dot_general(yp[v, i], split(d), NT, preferred_element_type=F32)
-
-    def inner_step(i, acc):
-        for v in range(V):
-            acc = acc + axial_row(v, i)
+    def axial_step(v, acc):
+        for i in range(NI // 2):
+            pair = []
+            for r in (2 * i, 2 * i + 1):
+                total = dt[v, r]
+                for k, cf in zip((1, 2, 3), COEFFS):
+                    if r >= k:
+                        total = total + cf * fs[v, r - k]
+                    if r + k < NI:
+                        total = total - cf * fs[v, r + k]
+                dt[v, r] = total
+                pair.append(total)
+            acc = acc + lax.dot_general(yp[v, i], split(jnp.concatenate(pair, axis=1)), NT, preferred_element_type=F32)
         return acc
 
-    acc = lax.fori_loop(3, NI - 3, inner_step, jnp.zeros((2 * S, 2 * S), F32), unroll=2)
+    acc = lax.fori_loop(0, V, axial_step, jnp.zeros((2 * S, 2 * S), F32))
+
+    def halo_flux(side):
+        keep = jnp.full((S, NL), jnp.where(side == 0, jnp.where(sp > 0, 1, 0), jnp.where(sp < nsp - 1, 1, 0))) > 0
+        for j in range(3):
+            axial = flux_axial([ha[side, v, j] for v in range(V)])
+            for v in range(V):
+                fh[side, v, j] = jnp.where(keep, axial[v], 0.0)
+        return keep
+
+    lower = jnp.where(c == 0, 1.0, 0.0)
+
+    def cross_coeff(mine, theirs):
+        if mine == theirs:
+            return COEFFS[2]
+        if mine < theirs:
+            return COEFFS[2 - theirs + mine] * lower
+        return COEFFS[2 - mine + theirs] * (1.0 - lower)
+
+    first_halo.wait()
+    keep = halo_flux(c)
+    sign = 2.0 * lower - 1.0
+
+    def cross_step(v, acc):
+        theirs = [fh[c, v, j] for j in range(3)]
+        mine = [fs[v, c * (NI - 3) + j] for j in range(3)]
+        for p in range(3):
+            near_mine = sign * sum(cross_coeff(p, j) * theirs[j] for j in range(3))
+            near_theirs = -sign * sum(cross_coeff(j, p) * mine[j] for j in range(3))
+            left = jnp.concatenate([y[v, c * (NI - 3) + p], jnp.where(keep, ha[c, v, p], 0.0)], axis=1)
+            right = jnp.concatenate([near_mine, near_theirs], axis=1)
+            acc = acc + lax.dot_general(split(left), split(right), NT, preferred_element_type=F32)
+        return acc
+
+    acc = lax.fori_loop(0, V, cross_step, acc)
+    start_core(1, pack(acc, tmp))
 
     tile = end_plane(0)
     if far:
         pl.semaphore_wait(known.at[1], far)
     start_deep(0, tile)
-
-    for h in halo:
-        h.wait()
-    for side in range(2):
-        keep = jnp.full((S, NL), jnp.where(sp > 0, 1, 0) if side == 0 else jnp.where(sp < nsp - 1, 1, 0)) > 0
-        for j in range(3):
-            axial = flux_axial([ha[side, v, j] for v in range(V)])
-            for v in range(V):
-                fs[v, j + (NI + 3) * side] = jnp.where(keep, axial[v], 0.0)
-    for i in EDGE:
-        acc = inner_step(i, acc)
-    start_core(1, pack(acc, tmp))
     start_plane(1, end_core(1))
+
+    other_halo.wait()
+    halo_flux(1 - c)
+    for v in range(V):
+        for p in range(3):
+            low_row, high_row = dt[v, p], dt[v, NI - 3 + p]
+            for j in range(p, 3):
+                low_row = low_row + COEFFS[2 - j + p] * fh[0, v, j]
+            for j in range(p + 1):
+                high_row = high_row - COEFFS[2 - p + j] * fh[1, v, j]
+            dt[v, p], dt[v, NI - 3 + p] = low_row, high_row
     for s in range(S):
         pltpu.make_async_copy(dt.at[:, :, s, :], div.at[s], out_sem.at[0]).start()
     start_deep(1, end_plane(1))
@@ -300,9 +339,10 @@
     lhs = jnp.concatenate([high, (twice - high.astype(F32)).astype(BF16)], axis=0)[:, 0 : 2 * S]
 
     def mode_step(v, carry):
-        for i in range(NI):
+        for i in range(NI // 2):
             out = jnp.dot(lhs, yp[v, i], preferred_element_type=F32)
-            mt[v, i] = out[0:S] + out[S : 2 * S]
+            out = out[0:S] + out[S : 2 * S]
+            mt[v, 2 * i], mt[v, 2 * i + 1] = out[:, 0:NL], out[:, NL : 2 * NL]
         return carry
 
     lax.fori_loop(0, V, mode_step, 0)
@@ -338,8 +378,9 @@
         out_specs=[vmem, vmem, vmem],
         scratch_shapes=[
             pltpu.VMEM((V, NI, S, NL), F32),
-            pltpu.VMEM((V, NI, 2 * S, NL), BF16),
-            pltpu.VMEM((V, NI + 6, S, NL), F32),
+            pltpu.VMEM((V, NI // 2, 2 * S, 2 * NL), BF16),
+            pltpu.VMEM((V, NI, S, NL), F32),
+            pltpu.VMEM((2, V, 3, S, NL), F32),
             pltpu.VMEM((V, NI, S, NL), F32),
             pltpu.VMEM((V, NI, S, NL), F32),
             pltpu.VMEM((V, NI, S, 2 * NL), BF16),

time: 39.2 us -> 40.3 us (1.028)
  Pallas kernels: 38.4 us -> 39.4 us
    pallas_call x1, Pallas kernels: 36.8 us -> 37.9 us  [per_device(): pl.pallas_call(functools.partial(main_kernel, dims, count), out_shape=[pl...]
where the time goes in v4:
time: 40.3 us; the launch traced here: 40.1 us
  Pallas kernels  39.4 us (98%)
  between operations  0.64 us (2%)
    pallas_call x1, Pallas kernels, per_device(): pl.pallas_call(functools.partial(main_kernel, dims, count), out_shape=[pl...  37.9 us
    pallas_call x1, Pallas kernels, per_device(): pl.pallas_call(write_kernel, out_shape=[jax.ShapeDtypeStruct(big, F32), j...  1.52 us

profile of v4, /device:TPU:1, one launch (start us, length us, event | category | flops | bytes accessed | tf_op | source)
XLA Modules:
  0.0 40.1 jit_solution(13041949738108494096)
XLA Ops:
  0.6 37.9 %shard_map.38 = (f32[32,5,16,128]{3,2,1,0:T(8,128)S(1)}, f32[32,5,16,128]{3,2,1,0:T(8,128)S(1)}, f32[32,32]{1,0:T(8,128)S(1)}) custom-call(f32[32,5,16,128]{3,2,1,0:T(8,128)} %snap.1), custom_call_target="tpu_custom_call" | custom-call | tf_op jit(solution)/shard_map/pallas_call | solution.py:374
  38.6 1.5 %shard_map.39 = (f32[32,5,16,128]{3,2,1,0:T(8,128)}, f32[32,5,16,128]{3,2,1,0:T(8,128)}, f32[32,32]{1,0:T(8,128)}) custom-call(f32[32,5,16,128]{3,2,1,0:T(8,128)S(1)} %get-tuple-element.6.modes, f32[32,5,16,128]{3,2,1,0:T(8,128)S(1)} %get-tuple-element.7.div, f32[32,32]{1,0:T(8,128)S(1)} %get-tuple-element.8.red), custom_call_target="tpu_custom_call" | custom-call | tf_op jit(solution)/shard_map/pallas_call | solution.py:405

commit v5 on v4

--- a/solution.py
+++ b/solution.py
@@ -11,7 +11,8 @@
 F32 = jnp.float32
 BF16 = jnp.bfloat16
 HIGHEST = lax.Precision.HIGHEST
-COEFFS = (0.75, -0.15, 1.0 / 60.0)
+SIXTIETHS = (45.0, -9.0, 1.0)
+SCALE = 1.0 / 60.0
 S, V, NI, NL = 32, 5, 16, 128
 NT = (((1,), (1,)), ((), ()))
 TN = (((0,), (0,)), ((), ()))
@@ -23,9 +24,9 @@
     return jnp.concatenate([high, low], axis=0)
 
 
-def high_low(a):
-    high = a.astype(BF16)
-    return jnp.concatenate([high, (a - high.astype(F32)).astype(BF16)], axis=1)
+def parts(a):
+    high = a.astype(BF16).astype(F32)
+    return high, a - high
 
 
 def flux_state(q):
@@ -57,12 +58,17 @@
     return axial, radial
 
 
-def pack(acc, tmp):
+def pack(acc, tmp, more=None):
     tmp[...] = jnp.zeros_like(tmp)
     tmp[:, 0:64] = acc
     full = tmp[...]
     rows = full[0:32] + full[32:64]
     both = rows + pltpu.roll(rows, NL - 32, axis=1)
+    if more is not None:
+        both = both + more[0:S]
+        for r in (1, 2, 3):
+            both = both + pltpu.roll(more[S * r : S * (r + 1)], NL - S * r, axis=1)
+        both = both * SCALE
     lane = lax.broadcasted_iota(jnp.int32, (8, NL), 1)
     out = jnp.zeros((8, NL), F32)
     for r in range(4):
@@ -94,7 +100,7 @@
     return sorted({d % n for k in steps for d in (k, -k)} - {0})
 
 
-def main_kernel(dims, count, snap, modes, div, red, y, yp, fs, fh, dt, mt, gs, gt, ed, ha, hr, tmp, sb, rc, rp, rz, known, load_sem, out_sem, send, recv):
+def main_kernel(dims, count, snap, modes, div, red, y, yp, fs, fh, dt, mt, gs, gt, gz, ed, ha, hr, tmp, sb, rc, rp, rz, known, load_sem, out_sem, send, recv):
     nz, nx, ny = dims
     nsp, nra = nz * nx, ny * 2
     sp, ra = lax.axis_index("space"), lax.axis_index("radial")
@@ -139,7 +145,14 @@
 
     first_halo = remote(y.at[:, pl.ds((1 - c) * (NI - 3), 3)], ha.at[c], 0, ((sp + nsp + 1 - 2 * c) % nsp, ra))
     other_halo = remote(y.at[:, pl.ds(c * (NI - 3), 3)], ha.at[1 - c], 1, ((sp + nsp - 1 + 2 * c) % nsp, ra))
-    first_halo.start()
+    has_behind, has_ahead = jnp.where(sp > 0, 1, 0), jnp.where(sp < nsp - 1, 1, 0)
+    first_sent = jnp.where(c == 0, has_ahead, has_behind) > 0
+    first_due = jnp.where(c == 0, has_behind, has_ahead) > 0
+
+    @pl.when(first_sent)
+    def _():
+        first_halo.start()
+
     near = signal(known.at[0], line_x + skip_z)
 
     def start_core(k, tile):
@@ -164,10 +177,10 @@
         landed = buf.at[k, 0 : n - 1]
         pltpu.make_async_copy(landed, landed, recv.at[4 + 3 * k + stage]).wait()
         pltpu.make_async_copy(landed, landed, send.at[4 + 3 * k + stage]).wait()
-        parts = [buf[k, i] for i in range(n)]
-        while len(parts) > 1:
-            parts = [parts[i] + parts[i + 1] for i in range(0, len(parts), 2)]
-        return parts[0]
+        terms = [buf[k, i] for i in range(n)]
+        while len(terms) > 1:
+            terms = [terms[i] + terms[i + 1] for i in range(0, len(terms), 2)]
+        return terms[0]
 
     def start_plane(k, tile):
         start_many(k, 1, rp, x * ny + yy, nx * ny, nth_plane, tile)
@@ -223,53 +236,34 @@
     pl.semaphore_wait(known.at[0], near)
     start_plane(0, tile)
     far = signal(known.at[1], far_z)
-    other_halo.start()
+
+    @pl.when(first_due)
+    def _():
+        other_halo.start()
+
     shift = lax.broadcasted_iota(jnp.int32, (NL, NL), 1) - lax.broadcasted_iota(jnp.int32, (NL, NL), 0)
     matrix = jnp.zeros((NL, NL), F32)
-    for k, cf in zip((1, 2, 3), COEFFS):
+    for k, cf in zip((1, 2, 3), SIXTIETHS):
         matrix = jnp.where(shift == k, cf, jnp.where(shift == -k, -cf, matrix))
-    matrix = high_low(matrix)
-    matrix = jnp.concatenate([matrix, matrix], axis=0)
+    matrix = jnp.concatenate([matrix, matrix], axis=0).astype(BF16)
 
     def radial_step(v, carry):
         out = jnp.dot(gs[v].reshape(NI * S, 2 * NL), matrix, preferred_element_type=F32)
-        dt[v] = (out[:, 0:NL] + out[:, NL : 2 * NL]).reshape(NI, S, NL)
+        dt[v] = out.reshape(NI, S, NL)
         return carry
 
     lax.fori_loop(0, V, radial_step, 0)
-
-    for h in radial_halo:
-        h.wait()
-    step = jnp.where(row8 < 3, row8 + NL - lane8, lane8 + 6 - row8)
-    weight = jnp.zeros((8, NL), F32)
-    for k, cf in zip((1, 2, 3), COEFFS):
-        weight = jnp.where(step == k, cf, weight)
-    weight = jnp.where(row8 < 6, jnp.where(row8 < 3, -weight, weight), 0.0)
-    weights = high_low(jnp.concatenate([weight] * 16, axis=0))
-    group = (lax.broadcasted_iota(jnp.int32, (NL, 2 * NL), 0) // 8) % 8
-    valid = jnp.where(row8 < 3, jnp.where(ra < nra - 1, 1, 0), jnp.where((row8 < 6) & (ra > 0), 1, 0)) > 0
-    blank = jnp.zeros((24, NL), F32)
-    for j in range(4):
-        cells = [jnp.where(row8 < 3, hr[1, v, j], hr[0, v, j]) for v in range(V)]
-        cells[0] = jnp.where(row8 < 6, cells[0], 1.0)
-        rows = jnp.concatenate([jnp.where(valid, g, 0.0) for g in flux_radial(cells)], axis=0)
-        high = rows.astype(BF16).astype(F32)
-        rows = jnp.concatenate([high, blank, rows - high, blank], axis=0)
-        gt[j] = rows.T.astype(BF16)
-    for v in range(V):
-        out = jnp.dot(gt[...].reshape(NI * S, NL), jnp.where(group == v, weights, 0.0).astype(BF16), preferred_element_type=F32)
-        dt[v] = dt[v] + (out[:, 0:NL] + out[:, NL : 2 * NL]).reshape(NI, S, NL)
 
     def axial_step(v, acc):
         for i in range(NI // 2):
             pair = []
             for r in (2 * i, 2 * i + 1):
                 total = dt[v, r]
-                for k, cf in zip((1, 2, 3), COEFFS):
-                    if r >= k:
-                        total = total + cf * fs[v, r - k]
-                    if r + k < NI:
-                        total = total - cf * fs[v, r + k]
+                for k, cf in zip((1, 2, 3), SIXTIETHS):
+                    if k <= r < NI - k:
+                        total = total + cf * (fs[v, r - k] - fs[v, r + k])
+                    else:
+                        total = total + cf * fs[v, r - k] if r >= k else total - cf * fs[v, r + k]
                 dt[v, r] = total
                 pair.append(total)
             acc = acc + lax.dot_general(yp[v, i], split(jnp.concatenate(pair, axis=1)), NT, preferred_element_type=F32)
@@ -289,12 +283,21 @@
 
     def cross_coeff(mine, theirs):
         if mine == theirs:
-            return COEFFS[2]
+            return SIXTIETHS[2]
         if mine < theirs:
-            return COEFFS[2 - theirs + mine] * lower
-        return COEFFS[2 - mine + theirs] * (1.0 - lower)
-
-    first_halo.wait()
+            return SIXTIETHS[2 - theirs + mine] * lower
+        return SIXTIETHS[2 - mine + theirs] * (1.0 - lower)
+
+    def land(copy, due, side):
+        @pl.when(due)
+        def _():
+            copy.wait_recv()
+
+        @pl.when(jnp.logical_not(due))
+        def _():
+            ha[side] = jnp.ones((V, 3, S, NL), F32)
+
+    land(first_halo, first_due, c)
     keep = halo_flux(c)
     sign = 2.0 * lower - 1.0
 
@@ -310,7 +313,31 @@
         return acc
 
     acc = lax.fori_loop(0, V, cross_step, acc)
-    start_core(1, pack(acc, tmp))
+
+    for h in radial_halo:
+        h.wait()
+    edge = lax.broadcasted_iota(jnp.int32, (8 * V, 8 * V), 0)
+    ghost = lax.broadcasted_iota(jnp.int32, (8 * V, 8 * V), 1)
+    same, edge, ghost = edge // 8 == ghost // 8, edge % 8, ghost % 8
+    high_side = jnp.where((ghost < 3) & (edge >= 3) & (edge < 6), 6 + ghost - edge, 0)
+    low_side = jnp.where((ghost >= 3) & (ghost < 6) & (edge < 3), 6 + edge - ghost, 0)
+    link = jnp.zeros((8 * V, 8 * V), F32)
+    for k, cf in zip((1, 2, 3), SIXTIETHS):
+        link = jnp.where(same & (low_side == k), cf, jnp.where(same & (high_side == k), -cf, link))
+    valid = jnp.where(row8 < 3, jnp.where(ra < nra - 1, 1, 0), jnp.where((row8 < 6) & (ra > 0), 1, 0)) > 0
+    blank = jnp.zeros((8, NL), F32)
+    more = jnp.zeros((NL, NL), F32)
+    for j in range(4):
+        cells = [jnp.where(row8 < 3, hr[1, v, j], hr[0, v, j]) for v in range(V)]
+        cells[0] = jnp.where(row8 < 6, cells[0], 1.0)
+        ghosts = jnp.concatenate([jnp.where(valid, g, 0.0) for g in flux_radial(cells)], axis=0)
+        gz[j] = ghosts
+        added = parts(jnp.dot(link, ghosts, preferred_element_type=F32, precision=HIGHEST))
+        mine = parts(jnp.concatenate([ed[v, j] for v in range(V)], axis=0))
+        left = jnp.concatenate([a for m in (0, 1, 0, 1) for a in (mine[m], blank)], axis=0)
+        right = jnp.concatenate([a for m in (0, 0, 1, 1) for a in (added[m], blank)], axis=0)
+        more = more + lax.dot_general(left.astype(BF16), right.astype(BF16), TN, preferred_element_type=F32)
+    start_core(1, pack(acc, tmp, more))
 
     tile = end_plane(0)
     if far:
@@ -318,15 +345,39 @@
     start_deep(0, tile)
     start_plane(1, end_core(1))
 
-    other_halo.wait()
+    step = jnp.where(row8 < 3, row8 + NL - lane8, lane8 + 6 - row8)
+    weight = jnp.zeros((8, NL), F32)
+    for k, cf in zip((1, 2, 3), SIXTIETHS):
+        weight = jnp.where(step == k, cf, weight)
+    weight = jnp.where(row8 < 6, jnp.where(row8 < 3, -weight, weight), 0.0)
+    weights = jnp.concatenate([weight] * 16, axis=0)
+    group = (lax.broadcasted_iota(jnp.int32, (NL, NL), 0) // 8) % 8
+    blank = jnp.zeros((24, NL), F32)
+    for j in range(4):
+        high, low = parts(gz[j])
+        gt[j] = jnp.concatenate([high, blank, low, blank], axis=0).T.astype(BF16)
+    for v in range(V):
+        out = jnp.dot(gt[...].reshape(NI * S, NL), jnp.where(group == v, weights, 0.0).astype(BF16), preferred_element_type=F32)
+        dt[v] = (dt[v] + out.reshape(NI, S, NL)) * SCALE
+
+    land(other_halo, first_sent, 1 - c)
     halo_flux(1 - c)
+
+    @pl.when(first_sent)
+    def _():
+        first_halo.wait_send()
+
+    @pl.when(first_due)
+    def _():
+        other_halo.wait_send()
+
     for v in range(V):
         for p in range(3):
             low_row, high_row = dt[v, p], dt[v, NI - 3 + p]
             for j in range(p, 3):
-                low_row = low_row + COEFFS[2 - j + p] * fh[0, v, j]
+                low_row = low_row + SCALE * SIXTIETHS[2 - j + p] * fh[0, v, j]
             for j in range(p + 1):
-                high_row = high_row - COEFFS[2 - p + j] * fh[1, v, j]
+                high_row = high_row - SCALE * SIXTIETHS[2 - p + j] * fh[1, v, j]
             dt[v, p], dt[v, NI - 3 + p] = low_row, high_row
     for s in range(S):
         pltpu.make_async_copy(dt.at[:, :, s, :], div.at[s], out_sem.at[0]).start()
@@ -385,6 +436,7 @@
             pltpu.VMEM((V, NI, S, NL), F32),
             pltpu.VMEM((V, NI, S, 2 * NL), BF16),
             pltpu.VMEM((4, NL, NL), BF16),
+            pltpu.VMEM((4, 8 * V, NL), F32),
             pltpu.VMEM((V, 4, 8, NL), F32),
             pltpu.VMEM((2, V, 3, S, NL), F32),
             pltpu.VMEM((2, V, 4, 8, NL), F32),

time: 40.3 us -> 40.3 us (level)
  no operation moved by 1% of the time
where the time goes in v5:
time: 40.3 us; the launch traced here: 40.1 us
  Pallas kernels  39.4 us (98%)
  between operations  0.64 us (2%)
    pallas_call x1, Pallas kernels, per_device(): pl.pallas_call(functools.partial(main_kernel, dims, count), out_shape=[pl...  37.9 us
    pallas_call x1, Pallas kernels, per_device(): pl.pallas_call(write_kernel, out_shape=[jax.ShapeDtypeStruct(big, F32), j...  1.52 us

profile of v5, /device:TPU:1, one launch (start us, length us, event | category | flops | bytes accessed | tf_op | source)
XLA Modules:
  0.0 40.1 jit_solution(11626448151721588093)
XLA Ops:
  0.6 37.9 %shard_map.38 = (f32[32,5,16,128]{3,2,1,0:T(8,128)S(1)}, f32[32,5,16,128]{3,2,1,0:T(8,128)S(1)}, f32[32,32]{1,0:T(8,128)S(1)}) custom-call(f32[32,5,16,128]{3,2,1,0:T(8,128)} %snap.1), custom_call_target="tpu_custom_call" | custom-call | tf_op jit(solution)/shard_map/pallas_call | solution.py:425
  38.6 1.5 %shard_map.39 = (f32[32,5,16,128]{3,2,1,0:T(8,128)}, f32[32,5,16,128]{3,2,1,0:T(8,128)}, f32[32,32]{1,0:T(8,128)}) custom-call(f32[32,5,16,128]{3,2,1,0:T(8,128)S(1)} %get-tuple-element.6.modes, f32[32,5,16,128]{3,2,1,0:T(8,128)S(1)} %get-tuple-element.7.div, f32[32,32]{1,0:T(8,128)S(1)} %get-tuple-element.8.red), custom_call_target="tpu_custom_call" | custom-call | tf_op jit(solution)/shard_map/pallas_call | solution.py:457

commit v6 on v5

--- a/solution.py
+++ b/solution.py
@@ -100,7 +100,7 @@
     return sorted({d % n for k in steps for d in (k, -k)} - {0})
 
 
-def main_kernel(dims, count, snap, modes, div, red, y, yp, fs, fh, dt, mt, gs, gt, gz, ed, ha, hr, tmp, sb, rc, rp, rz, known, load_sem, out_sem, send, recv):
+def main_kernel(dims, count, snap, modes, div, red, y, yp, fs, fh, dt, gs, gt, gz, ed, ha, hr, tmp, sb, rc, rp, rz, known, load_sem, send, recv):
     nz, nx, ny = dims
     nsp, nra = nz * nx, ny * 2
     sp, ra = lax.axis_index("space"), lax.axis_index("radial")
@@ -152,6 +152,10 @@
     @pl.when(first_sent)
     def _():
         first_halo.start()
+
+    @pl.when(first_due)
+    def _():
+        other_halo.start()
 
     near = signal(known.at[0], line_x + skip_z)
 
@@ -236,11 +240,6 @@
     pl.semaphore_wait(known.at[0], near)
     start_plane(0, tile)
     far = signal(known.at[1], far_z)
-
-    @pl.when(first_due)
-    def _():
-        other_halo.start()
-
     shift = lax.broadcasted_iota(jnp.int32, (NL, NL), 1) - lax.broadcasted_iota(jnp.int32, (NL, NL), 0)
     matrix = jnp.zeros((NL, NL), F32)
     for k, cf in zip((1, 2, 3), SIXTIETHS):
@@ -359,6 +358,8 @@
     for v in range(V):
         out = jnp.dot(gt[...].reshape(NI * S, NL), jnp.where(group == v, weights, 0.0).astype(BF16), preferred_element_type=F32)
         dt[v] = (dt[v] + out.reshape(NI, S, NL)) * SCALE
+        for i in range(3, NI - 3):
+            div[pl.ds(v * NI + i, S, stride=V * NI), :] = dt[v, i]
 
     land(other_halo, first_sent, 1 - c)
     halo_flux(1 - c)
@@ -378,9 +379,8 @@
                 low_row = low_row + SCALE * SIXTIETHS[2 - j + p] * fh[0, v, j]
             for j in range(p + 1):
                 high_row = high_row - SCALE * SIXTIETHS[2 - p + j] * fh[1, v, j]
-            dt[v, p], dt[v, NI - 3 + p] = low_row, high_row
-    for s in range(S):
-        pltpu.make_async_copy(dt.at[:, :, s, :], div.at[s], out_sem.at[0]).start()
+            div[pl.ds(v * NI + p, S, stride=V * NI), :] = low_row
+            div[pl.ds(v * NI + NI - 3 + p, S, stride=V * NI), :] = high_row
     start_deep(1, end_plane(1))
     gram = unpack(end_deep(0)) / count
     low = inverse_factor(gram)
@@ -393,17 +393,14 @@
         for i in range(NI // 2):
             out = jnp.dot(lhs, yp[v, i], preferred_element_type=F32)
             out = out[0:S] + out[S : 2 * S]
-            mt[v, 2 * i], mt[v, 2 * i + 1] = out[:, 0:NL], out[:, NL : 2 * NL]
+            for r in range(2):
+                modes[pl.ds(v * NI + 2 * i + r, S, stride=V * NI), :] = out[:, r * NL : (r + 1) * NL]
         return carry
 
     lax.fori_loop(0, V, mode_step, 0)
-    for s in range(S):
-        pltpu.make_async_copy(mt.at[:, :, s, :], modes.at[s], out_sem.at[1]).start()
     cross = unpack(end_deep(1))
     root = jnp.sqrt(jnp.full((S, S), count, F32))
     red[...] = jnp.dot(low[:, 0:S], cross[:, 0:S], preferred_element_type=F32, precision=HIGHEST) / root
-    pltpu.make_async_copy(dt, dt, out_sem.at[0]).wait()
-    pltpu.make_async_copy(mt, mt, out_sem.at[1]).wait()
 
 
 def write_kernel(modes, div, red, modes_out, div_out, red_out, sem):
@@ -420,7 +417,7 @@
     count = float(V * NI * nz * nx * NL * ny * 2)
     vmem = pl.BlockSpec(memory_space=pltpu.VMEM)
     hbm = pl.BlockSpec(memory_space=pl.ANY)
-    big = (S, V, NI, NL)
+    big = (S * V * NI, NL)
     dma = pltpu.SemaphoreType.DMA
     modes, div, red = pl.pallas_call(
         functools.partial(main_kernel, dims, count),
@@ -432,7 +429,6 @@
             pltpu.VMEM((V, NI // 2, 2 * S, 2 * NL), BF16),
             pltpu.VMEM((V, NI, S, NL), F32),
             pltpu.VMEM((2, V, 3, S, NL), F32),
-            pltpu.VMEM((V, NI, S, NL), F32),
             pltpu.VMEM((V, NI, S, NL), F32),
             pltpu.VMEM((V, NI, S, 2 * NL), BF16),
             pltpu.VMEM((4, NL, NL), BF16),
@@ -447,7 +443,6 @@
             pltpu.VMEM((2, nz, 8, NL), F32),
             pltpu.SemaphoreType.REGULAR((2,)),
             dma,
-            dma((2,)),
             dma((10,)),
             dma((10,)),
         ],
@@ -461,7 +456,7 @@
         out_specs=[hbm, hbm, hbm],
         scratch_shapes=[dma((3,))],
     )(*pinned)
-    return modes, div, red
+    return modes.reshape(snapshots.shape), div.reshape(snapshots.shape), red
 
 
 def solution(mesh):

time: 40.3 us -> 38.6 us (0.958); the launches traced: 40.1 us -> 37.9 us
  Pallas kernels: 39.4 us -> 37.3 us
    pallas_call x1, Pallas kernels: 37.9 us -> 35.8 us  [per_device(): pl.pallas_call(functools.partial(main_kernel, dims, count), out_shape=[pl...]
where the time goes in v6:
time: 38.6 us; the launch traced here: 37.9 us
  Pallas kernels  37.3 us (97%)
  between operations  0.64 us (2%)
    pallas_call x1, Pallas kernels, per_device(): pl.pallas_call(functools.partial(main_kernel, dims, count), out_shape=[pl...  35.8 us
    pallas_call x1, Pallas kernels, per_device(): pl.pallas_call(write_kernel, out_shape=[jax.ShapeDtypeStruct(big, F32), j...  1.52 us

profile of v6, /device:TPU:1, one launch (start us, length us, event | category | flops | bytes accessed | tf_op | source)
XLA Modules:
  0.0 37.9 jit_solution(8245579898626940147)
XLA Ops:
  0.6 35.8 %shard_map.38 = (f32[2560,128]{1,0:T(8,128)S(1)}, f32[2560,128]{1,0:T(8,128)S(1)}, f32[32,32]{1,0:T(8,128)S(1)}) custom-call(f32[32,5,16,128]{3,2,1,0:T(8,128)} %snap.1), custom_call_target="tpu_custom_call" | custom-call | tf_op jit(solution)/shard_map/pallas_call | solution.py:422
  36.4 1.5 %shard_map.39 = (f32[2560,128]{1,0:T(8,128)}, f32[2560,128]{1,0:T(8,128)}, f32[32,32]{1,0:T(8,128)}) custom-call(f32[2560,128]{1,0:T(8,128)S(1)} %get-tuple-element.9.modes, f32[2560,128]{1,0:T(8,128)S(1)} %get-tuple-element.10.div, f32[32,32]{1,0:T(8,128)S(1)} %get-tuple-element.11.red), custom_call_target="tpu_custom_call" | custom-call | tf_op jit(solution)/shard_map/pallas_call | solution.py:452

commit v7 on v6

--- a/solution.py
+++ b/solution.py
@@ -135,68 +135,15 @@
         return len(targets)
 
     near = signal(barrier, [ahead_a, behind_a, ahead_r, behind_r, core] + near_z + line_x + line_y)
-    for s in range(S):
-        pltpu.make_async_copy(snap.at[s], y.at[:, :, s, :], load_sem).start()
-    pltpu.make_async_copy(y, y, load_sem).wait()
-    pl.semaphore_wait(barrier, near)
+    for v in range(V):
+        for s in range(S):
+            pltpu.make_async_copy(snap.at[s, v], y.at[v, :, s, :], load_sem.at[v]).start()
+
+    def loaded(v):
+        pltpu.make_async_copy(y.at[v], y.at[v], load_sem.at[v]).wait()
 
     def remote(src, dst, k, peer):
         return pltpu.make_async_remote_copy(src, dst, send.at[k], recv.at[k], device_id=peer, device_id_type=MESH)
-
-    first_halo = remote(y.at[:, pl.ds((1 - c) * (NI - 3), 3)], ha.at[c], 0, ((sp + nsp + 1 - 2 * c) % nsp, ra))
-    other_halo = remote(y.at[:, pl.ds(c * (NI - 3), 3)], ha.at[1 - c], 1, ((sp + nsp - 1 + 2 * c) % nsp, ra))
-    has_behind, has_ahead = jnp.where(sp > 0, 1, 0), jnp.where(sp < nsp - 1, 1, 0)
-    first_sent = jnp.where(c == 0, has_ahead, has_behind) > 0
-    first_due = jnp.where(c == 0, has_behind, has_ahead) > 0
-
-    @pl.when(first_sent)
-    def _():
-        first_halo.start()
-
-    @pl.when(first_due)
-    def _():
-        other_halo.start()
-
-    near = signal(known.at[0], line_x + skip_z)
-
-    def start_core(k, tile):
-        sb[3 * k] = tile
-        remote(sb.at[3 * k], rc.at[k], 4 + 3 * k, core).start()
-
-    def end_core(k):
-        remote(sb.at[3 * k], rc.at[k], 4 + 3 * k, core).wait()
-        return sb[3 * k] + rc[k]
-
-    def start_many(k, stage, buf, mine, n, target, tile):
-        sb[3 * k + stage] = tile
-        buf[k, mine] = tile
-
-        def send_one(i, carry):
-            remote(sb.at[3 * k + stage], buf.at[k, mine], 4 + 3 * k + stage, target(i)).start()
-            return carry
-
-        lax.fori_loop(0, n - 1, send_one, 0)
-
-    def end_many(k, stage, buf, n):
-        landed = buf.at[k, 0 : n - 1]
-        pltpu.make_async_copy(landed, landed, recv.at[4 + 3 * k + stage]).wait()
-        pltpu.make_async_copy(landed, landed, send.at[4 + 3 * k + stage]).wait()
-        terms = [buf[k, i] for i in range(n)]
-        while len(terms) > 1:
-            terms = [terms[i] + terms[i + 1] for i in range(0, len(terms), 2)]
-        return terms[0]
-
-    def start_plane(k, tile):
-        start_many(k, 1, rp, x * ny + yy, nx * ny, nth_plane, tile)
-
-    def end_plane(k):
-        return end_many(k, 1, rp, nx * ny)
-
-    def start_deep(k, tile):
-        start_many(k, 2, rz, z, nz, nth_deep, tile)
-
-    def end_deep(k):
-        return end_many(k, 2, rz, nz)
 
     row8 = lax.broadcasted_iota(jnp.int32, (8, NL), 0)
     lane8 = lax.broadcasted_iota(jnp.int32, (8, NL), 1)
@@ -219,7 +166,70 @@
             ed[v, j] = jnp.concatenate(edge, axis=1)
         return acc
 
-    acc = lax.fori_loop(0, V, gram_step, jnp.zeros((2 * S, 2 * S), F32))
+    acc = jnp.zeros((2 * S, 2 * S), F32)
+    for v in range(2):
+        loaded(v)
+        acc = gram_step(v, acc)
+    for v in range(2, V):
+        loaded(v)
+    pl.semaphore_wait(barrier, near)
+
+    first_halo = remote(y.at[:, pl.ds((1 - c) * (NI - 3), 3)], ha.at[c], 0, ((sp + nsp + 1 - 2 * c) % nsp, ra))
+    other_halo = remote(y.at[:, pl.ds(c * (NI - 3), 3)], ha.at[1 - c], 1, ((sp + nsp - 1 + 2 * c) % nsp, ra))
+    has_behind, has_ahead = jnp.where(sp > 0, 1, 0), jnp.where(sp < nsp - 1, 1, 0)
+    first_sent = jnp.where(c == 0, has_ahead, has_behind) > 0
+    first_due = jnp.where(c == 0, has_behind, has_ahead) > 0
+
+    @pl.when(first_sent)
+    def _():
+        first_halo.start()
+
+    @pl.when(first_due)
+    def _():
+        other_halo.start()
+
+    near = signal(known.at[0], line_x + skip_z)
+
+    def start_core(k, tile):
+        sb[3 * k] = tile
+        remote(sb.at[3 * k], rc.at[k], 4 + 3 * k, core).start()
+
+    def end_core(k):
+        remote(sb.at[3 * k], rc.at[k], 4 + 3 * k, core).wait()
+        return sb[3 * k] + rc[k]
+
+    def start_many(k, stage, buf, mine, n, target, tile):
+        sb[3 * k + stage] = tile
+        buf[k, mine] = tile
+
+        def send_one(i, carry):
+            remote(sb.at[3 * k + stage], buf.at[k, mine], 4 + 3 * k + stage, target(i)).start()
+            return carry
+
+        lax.fori_loop(0, n - 1, send_one, 0)
+
+    def end_many(k, stage, buf, n):
+        landed = buf.at[k, 0 : n - 1]
+        pltpu.make_async_copy(landed, landed, recv.at[4 + 3 * k + stage]).wait()
+        pltpu.make_async_copy(landed, landed, send.at[4 + 3 * k + stage]).wait()
+        terms = [buf[k, i] for i in range(n)]
+        while len(terms) > 1:
+            terms = [terms[i] + terms[i + 1] for i in range(0, len(terms), 2)]
+        return terms[0]
+
+    def start_plane(k, tile):
+        start_many(k, 1, rp, x * ny + yy, nx * ny, nth_plane, tile)
+
+    def end_plane(k):
+        return end_many(k, 1, rp, nx * ny)
+
+    def start_deep(k, tile):
+        start_many(k, 2, rz, z, nz, nth_deep, tile)
+
+    def end_deep(k):
+        return end_many(k, 2, rz, nz)
+
+    acc = lax.fori_loop(2, V, gram_step, acc)
     start_core(0, pack(acc, tmp))
     radial_halo = [remote(ed, hr.at[0], 2, ahead_r), remote(ed, hr.at[1], 3, behind_r)]
     for h in radial_halo:
@@ -442,7 +452,7 @@
             pltpu.VMEM((2, nx * ny, 8, NL), F32),
             pltpu.VMEM((2, nz, 8, NL), F32),
             pltpu.SemaphoreType.REGULAR((2,)),
-            dma,
+            dma((V,)),
             dma((10,)),
             dma((10,)),
         ],

time: 38.6 us -> 38.6 us (level)
  no operation moved by 1% of the time
where the time goes in v7:
time: 38.6 us; the launch traced here: 38.1 us
  Pallas kernels  37.4 us (97%)
  between operations  0.64 us (2%)
    pallas_call x1, Pallas kernels, per_device(): pl.pallas_call(functools.partial(main_kernel, dims, count), out_shape=[pl...  35.9 us
    pallas_call x1, Pallas kernels, per_device(): pl.pallas_call(write_kernel, out_shape=[jax.ShapeDtypeStruct(big, F32), j...  1.52 us

profile of v7, /device:TPU:1, one launch (start us, length us, event | category | flops | bytes accessed | tf_op | source)
XLA Modules:
  0.0 38.1 jit_solution(3082880075739018615)
XLA Ops:
  0.6 35.9 %shard_map.38 = (f32[2560,128]{1,0:T(8,128)S(1)}, f32[2560,128]{1,0:T(8,128)S(1)}, f32[32,32]{1,0:T(8,128)S(1)}) custom-call(f32[32,5,16,128]{3,2,1,0:T(8,128)} %snap.1), custom_call_target="tpu_custom_call" | custom-call | tf_op jit(solution)/shard_map/pallas_call | solution.py:432
  36.5 1.5 %shard_map.39 = (f32[2560,128]{1,0:T(8,128)}, f32[2560,128]{1,0:T(8,128)}, f32[32,32]{1,0:T(8,128)}) custom-call(f32[2560,128]{1,0:T(8,128)S(1)} %get-tuple-element.9.modes, f32[2560,128]{1,0:T(8,128)S(1)} %get-tuple-element.10.div, f32[32,32]{1,0:T(8,128)S(1)} %get-tuple-element.11.red), custom_call_target="tpu_custom_call" | custom-call | tf_op jit(solution)/shard_map/pallas_call | solution.py:462
